TPU v7x, 32 devices: a whole 2x2x4 slice. The times are simulated.
32 devices in a mesh: mp: 2 (over y), fsdp: 8 (over z, core), tp: 2 (over x).
Axes of the slice: x: 2, y: 2, z: 4, core: 2. Of those that a mesh axis runs over, the one named last changes fastest.
Arguments:
- hidden: bfloat16 [2, 1280, 5120], P('mp', 'fsdp'), may hold values from -6 to 6
- live_weight: bfloat16 [2, 5120, 1024], P('mp', 'fsdp', 'tp'), may hold values from -0.078125 to 0.078125
- stale_weight: bfloat16 [2, 5120, 1024], P('mp', 'fsdp', 'tp'), may hold values from -0.078125 to 0.078125
- match: int32 [2, 1280], P('mp', 'fsdp'), may hold values from 0 to 159, as said below
Outputs:
- hidden_grad: bfloat16 [2, 1280, 5120], P('mp', 'fsdp', 'tp')
Inputs may be any that keep to these rules, and one draw needn't show every extreme that they name: Within each model's block of 160 rows, match is a permutation of 0 to 159, and the two models' permutations of a block are inverse to each other.
All inputs are finite; a program needn't handle non-finite values.
Results may differ from a plain program's by a relative error of at most 0.0061.
Values may be sent and summed in bfloat16 or wider, within the bound.
No kernel may reach another device: no remote copies, remote signals or barrier semaphores. Data moves between devices by JAX's collectives and lax.ppermute only.
A program may use at most 64 MiB of HBM per device.

v0:
```python
import jax
import jax.numpy as jnp
from jax import lax
from jax.sharding import PartitionSpec as P


def partner(block, axis, apart):
    count = lax.axis_size(axis)
    route = []
    for low in range(count):
        high = low | 1 << apart
        if high != low and high < count:
            route += [(low, high), (high, low)]
    return lax.ppermute(block, axis, route)


def shards(hidden, live_weight, stale_weight, match):
    hidden_rows = hidden[0]
    live_full = lax.all_gather(live_weight[0], "fsdp", axis=0, tiled=True)
    student = jnp.dot(hidden_rows, live_full, preferred_element_type=jnp.float32)
    stale_piece = stale_weight[0]
    teacher = jnp.dot(
        hidden_rows,
        lax.all_gather(stale_piece, "fsdp", axis=0, tiled=True),
        preferred_element_type=jnp.float32,
    ).astype(jnp.bfloat16)
    teacher = partner(teacher, "mp", 0)
    target = jnp.take(teacher, match[0], axis=0)
    mismatch = (student - target.astype(jnp.float32)).astype(jnp.bfloat16)
    partial_value = lax.dot_general(
        mismatch, live_full, (((1,), (1,)), ((), ())), preferred_element_type=jnp.float32
    )
    summed = lax.psum_scatter(
        partial_value.astype(jnp.bfloat16), "tp", scatter_dimension=1, tiled=True
    )
    return summed[None]


def solution(mesh):
    in_specs = (
        P("mp", "fsdp", None),
        P("mp", "fsdp", "tp"),
        P("mp", "fsdp", "tp"),
        P("mp", "fsdp"),
    )
    out_specs = P("mp", "fsdp", "tp")
    return jax.shard_map(shards, mesh=mesh, in_specs=in_specs, out_specs=out_specs, check_vma=False)
```

profile of v0, /device:TPU:0, one launch (start us, length us, event | category | flops | bytes accessed | tf_op | source)
XLA Modules:
  0.0 164.6 jit_solution(195391604350372213)
XLA Ops:
  6.5 0.0 copy-start
  6.5 0.0 copy-start.1
  6.5 0.0 all-gather.7.cloned.1.call-start
  6.5 0.7 all-gather.7.cloned.1.call-update
  7.3 0.0 all-gather.5.cloned.1.call-start
  7.3 0.7 all-gather.5.cloned.1.call-update
  8.0 0.0 reduce-scatter.2.cloned.1.call-start
  8.1 0.7 compare_select_fusion
  8.7 59.0 %all-gather.7.cloned.1.call-done = bf16[1,5120,512]{2,1,0:T(8,128)(2,1)} async-done(((bf16[1,640,512]{2,1,0:T(8,128)(2,1)}), bf16[1,5120,512]{2,1,0:T(8,128)(2,1)}) %all-gather.7.cloned.1.call-update) | async-done | bytes 5242896 | tf_op jit(solution)/shard_map/all_gather | solution.py:24
  67.8 0.0 copy-done
  67.8 3.5 %fusion.7 = bf16[160,512]{1,0:T(8,128)(2,1)S(1)} fusion(bf16[1,5120,512]{2,1,0:T(8,128)(2,1)} %all-gather.7.cloned.1.call-done, bf16[1,160,5120]{2,1,0:T(8,128)(2,1)S(1)} %copy-done), kind=kOutput, calls=%fused_computation.9 | convolution fusion | flops 838942720 | bytes 7045120 | tf_op jit(solution)/shard_map/dot_general | solution.py:22
  71.3 1.5 collective-permute-start
  72.8 0.0 copy-done.1
  72.9 4.8 %collective-permute-done = bf16[160,512]{1,0:T(8,128)(2,1)S(1)} collective-permute-done((bf16[160,512]{1,0:T(8,128)(2,1)S(1)}, bf16[160,512]{1,0:T(8,128)(2,1)S(1)}, u32[]{:S(2)}, u32[]{:S(2)}) %collective-permute-start) | collective-permute-done | bytes 163872 | tf_op jit(solution)/shard_map/ppermute | solution.py:14
  77.7 0.9 gather_fusion
  78.6 45.6 %all-gather.5.cloned.1.call-done = bf16[1,5120,512]{2,1,0:T(8,128)(2,1)} async-done(((bf16[1,640,512]{2,1,0:T(8,128)(2,1)}), bf16[1,5120,512]{2,1,0:T(8,128)(2,1)}) %all-gather.5.cloned.1.call-update) | async-done | bytes 5242896 | tf_op jit(solution)/shard_map/all_gather | solution.py:19
  124.3 8.1 %convolution_convert_fusion = bf16[160,5120]{1,0:T(8,128)(2,1)} fusion(bf16[1,5120,512]{2,1,0:T(8,128)(2,1)} %all-gather.5.cloned.1.call-done, bf16[1,160,5120]{2,1,0:T(8,128)(2,1)S(1)} %copy-done, bf16[160,512]{1,0:T(8,128)(2,1)S(1)} %gather_fusion, pred[160]{0:T(512)(128)(4,1)S(1)} %compare_and_fusion), kind=kOutput, calls=%fused_computation.1 | convolution fusion | flops 1678868480 | bytes 8683680 | tf_op jit(solution)/shard_map/dot_general | solution.py:30
  132.3 0.0 reduce-scatter.2.cloned.1.call-update
  132.4 25.7 %reduce-scatter.2.cloned.1.call-done = bf16[160,2560]{1,0:T(8,128)(2,1)} async-done(((bf16[160,5120]{1,0:T(8,128)(2,1)}), bf16[160,2560]{1,0:T(8,128)(2,1)}) %reduce-scatter.2.cloned.1.call-update) | async-done | bytes 819216 | tf_op jit(solution)/shard_map/reduce_scatter | solution.py:33
  (2 shorter events, 0.0 us)
Async XLA Ops:
  6.5 61.2 %copy-start = (bf16[1,160,5120]{2,1,0:T(8,128)(2,1)S(1)}, bf16[1,160,5120]{2,1,0:T(8,128)(2,1)}, u32[]{:S(2)}) copy-start(bf16[1,160,5120]{2,1,0:T(8,128)(2,1)} %param.4) | copy-start | bytes 4915204
  6.5 66.3 %copy-start.1 = (s32[1,160]{1,0:T(1,128)S(1)}, s32[1,160]{1,0:T(1,128)}, u32[]{:S(2)}) copy-start(s32[1,160]{1,0:T(1,128)} %param.7) | copy-start | bytes 1924
  6.5 61.2 %all-gather.7.cloned.1.call-start = ((), (), s32[]{:S(2)}) async-start(), calls=%async_computation.3 | async-start | bytes 5898240 | tf_op jit(solution)/shard_map/all_gather | solution.py:24
  7.3 117.0 %all-gather.5.cloned.1.call-start = ((), (), s32[]{:S(2)}) async-start(), calls=%async_computation.2 | async-start | bytes 5898240 | tf_op jit(solution)/shard_map/all_gather | solution.py:19
  8.0 150.1 %reduce-scatter.2.cloned.1.call-start = ((), (), s32[]{:S(2)}) async-start(), calls=%async_computation.1 | async-start | bytes 2457600 | tf_op jit(solution)/shard_map/reduce_scatter | solution.py:33
  71.3 6.4 %collective-permute-start = (bf16[160,512]{1,0:T(8,128)(2,1)S(1)}, bf16[160,512]{1,0:T(8,128)(2,1)S(1)}, u32[]{:S(2)}, u32[]{:S(2)}) collective-permute-start(bf16[160,512]{1,0:T(8,128)(2,1)S(1)} %fusion.7), channel_id=1, source_target_pairs={{0,16},{16,0},{1,17},{17,1},{2,18},{18,2},{3,19},{19,3},{4,20},{20... | collective-permute-start | bytes 491528 | tf_op jit(solution)/shard_map/ppermute | solution.py:14
Sparse Core Ops, SparseCore 0:
  9.0 58.7 all-gather.6
  69.4 54.8 all-gather.4
  132.5 25.5 reduce-scatter.1
where the time goes:
time: 165 us
  waiting for transfers between devices  137 us (83%)
  between operations  13.1 us (8%)
  matrix products  11.6 us (7%)
    all_gather x1, waiting for transfers between devices, shards(): lax.all_gather(stale_piece, 'fsdp', axis=0, tiled=True)  59 us
    all_gather x1, waiting for transfers between devices, shards(): live_full = lax.all_gather(live_weight[0], 'fsdp', axis=0, tiled=True)  45.6 us
    reduce_scatter x1, waiting for transfers between devices, shards(): lax.psum_scatter(partial_value.astype(jnp.bfloat16), 'tp', scatter_dimens...  25.7 us
    dot_general x1, matrix products, shards(): lax.dot_general(mismatch, live_full, (((1,), (1,)), ((), ())), preferred_...  8.07 us
    ppermute x1, waiting for transfers between devices, partner(): return lax.ppermute(block, axis, route)  4.84 us
    dot_general x1, matrix products, shards(): jnp.dot(hidden_rows, lax.all_gather(stale_piece, 'fsdp', axis=0, tiled=Tr...  3.5 us
  transfers between devices with their start and end apart: 4, of which 4 were waited for; matrix products, arithmetic and copies ran while one was open for 3% of the time, Pallas kernels for 0%

commit v1 on v0

--- a/solution.py
+++ b/solution.py
@@ -2,6 +2,27 @@
 import jax.numpy as jnp
 from jax import lax
 from jax.sharding import PartitionSpec as P
+
+
+def joined_along(pieces, dim):
+    lengths = list(pieces.shape[1:])
+    lengths[dim] *= pieces.shape[0]
+    return jnp.moveaxis(pieces, 0, dim).reshape(lengths)
+
+
+def grow_blocks(value, axis):
+    size, index = (lax.axis_size(axis), lax.axis_index(axis))
+    blocks, bit = (value[None], 1)
+    while bit < size:
+        theirs = lax.ppermute(blocks, axis, [(i, i ^ bit) for i in range(size)])
+        low = index & bit == 0
+        blocks = jnp.concatenate([jnp.where(low, blocks, theirs), jnp.where(low, theirs, blocks)])
+        bit *= 2
+    return blocks
+
+
+def doubled_up(x, axis, dim):
+    return joined_along(grow_blocks(x, axis), dim)
 
 
 def partner(block, axis, apart):
@@ -20,9 +41,7 @@
     student = jnp.dot(hidden_rows, live_full, preferred_element_type=jnp.float32)
     stale_piece = stale_weight[0]
     teacher = jnp.dot(
-        hidden_rows,
-        lax.all_gather(stale_piece, "fsdp", axis=0, tiled=True),
-        preferred_element_type=jnp.float32,
+        hidden_rows, doubled_up(stale_piece, "fsdp", 0), preferred_element_type=jnp.float32
     ).astype(jnp.bfloat16)
     teacher = partner(teacher, "mp", 0)
     target = jnp.take(teacher, match[0], axis=0)

time: 165 us -> 259 us (1.57)
  waiting for transfers between devices: 137 us -> 220 us
  other arithmetic: 0.7 us -> 7.82 us
  starting transfers between devices: 1.62 us -> 6.62 us
    ppermute x0 -> x3, waiting for transfers between devices: none -> 187 us  [grow_blocks(): theirs = lax.ppermute(blocks, axis, [(i, i ^ bit) for i in range(size)])]
    all_gather x1 -> x0, waiting for transfers between devices: 59 us -> none  [shards(): lax.all_gather(stale_piece, 'fsdp', axis=0, tiled=True)]
    all_gather x1, waiting for transfers between devices: 45.6 us -> 0.02 us  [shards(): live_full = lax.all_gather(live_weight[0], 'fsdp', axis=0, tiled=True)]
    select_n x0 -> x3, other arithmetic: none -> 5.29 us  [grow_blocks(): jnp.where(low, blocks, theirs)]
    ppermute x0 -> x3, starting transfers between devices: none -> 5.21 us  [grow_blocks(): theirs = lax.ppermute(blocks, axis, [(i, i ^ bit) for i in range(size)])]
  transfers between devices with their start and end apart: 4 -> 6, of which waited for: 4 -> 5; matrix products, arithmetic and copies ran while one was open for 3% -> 4% of each run, Pallas kernels for 0% -> 0%
where the time goes in v1:
time: 259 us
  waiting for transfers between devices  220 us (85%)
  between operations  13.5 us (5%)
  matrix products  9.06 us (3%)
  other arithmetic  7.82 us (3%)
  starting transfers between devices  6.62 us (3%)
    ppermute x3, waiting for transfers between devices, grow_blocks(): theirs = lax.ppermute(blocks, axis, [(i, i ^ bit) for i in range(size)])  187 us
    reduce_scatter x1, waiting for transfers between devices, shards(): lax.psum_scatter(partial_value.astype(jnp.bfloat16), 'tp', scatter_dimens...  27.7 us
    dot_general x1, matrix products, shards(): lax.dot_general(mismatch, live_full, (((1,), (1,)), ((), ())), preferred_...  8.05 us
    select_n x3, other arithmetic, grow_blocks(): jnp.where(low, blocks, theirs)  5.29 us
    ppermute x3, starting transfers between devices, grow_blocks(): theirs = lax.ppermute(blocks, axis, [(i, i ^ bit) for i in range(size)])  5.21 us
  transfers between devices with their start and end apart: 6, of which 5 were waited for; matrix products, arithmetic and copies ran while one was open for 4% of the time, Pallas kernels for 0%

profile of v1, /device:TPU:0, one launch (start us, length us, event | category | flops | bytes accessed | tf_op | source)
XLA Modules:
  0.0 258.6 jit_solution(16023624325789030812)
XLA Ops:
  6.5 0.0 copy-start
  6.5 0.0 all-gather.3.cloned.1.call-start
  6.5 0.7 all-gather.3.cloned.1.call-update
  7.3 0.0 reduce-scatter.2.cloned.1.call-start
  7.3 0.5 collective-permute-start
  7.8 1.9 collective-permute-done
  9.8 1.2 broadcast_select_fusion.5
  10.9 0.0 copy-start.2
  10.9 0.0 copy-start.3
  11.0 0.8 copy-done.2
  11.8 0.1 pad_maximum_fusion.2
  11.9 0.1 copy-done.3
  12.0 2.9 %collective-permute-start.1 = (bf16[2,640,512]{2,1,0:T(8,128)(2,1)S(1)}, bf16[2,640,512]{2,1,0:T(8,128)(2,1)}, u32[]{:S(2)}, u32[]{:S(2)}) collective-permute-start(bf16[2,640,512]{2,1,0:T(8,128)(2,1)S(1)} %pad_maximum_fusion.2), channel_id=1, source_target_pairs={{0,4},{2,6},{4,0},{6,2},{8,12},{10,14},{12,8},{14,10},{1,5},{3,7},... | collective-permute-start | bytes 3932168 | tf_op jit(solution)/shard_map/ppermute | solution.py:17
  14.9 71.3 %collective-permute-done.1 = bf16[2,640,512]{2,1,0:T(8,128)(2,1)} collective-permute-done((bf16[2,640,512]{2,1,0:T(8,128)(2,1)S(1)}, bf16[2,640,512]{2,1,0:T(8,128)(2,1)}, u32[]{:S(2)}, u32[]{:S(2)}) %collective-permute-start.1) | collective-permute-done | bytes 1310752 | tf_op jit(solution)/shard_map/ppermute | solution.py:17
  86.2 1.9 broadcast_select_fusion.3
  88.1 0.0 copy-start.1
  88.1 0.0 copy-start.4
  88.1 1.9 pad_maximum_fusion.1
  90.1 0.0 copy-done.1
  90.1 1.7 collective-permute-start.2
  91.8 0.0 copy-done.4
  91.8 114.1 %collective-permute-done.2 = bf16[4,640,512]{2,1,0:T(8,128)(2,1)} collective-permute-done((bf16[4,640,512]{2,1,0:T(8,128)(2,1)}, bf16[4,640,512]{2,1,0:T(8,128)(2,1)}, u32[]{:S(2)}, u32[]{:S(2)}) %collective-permute-start.2) | collective-permute-done | bytes 2621472 | tf_op jit(solution)/shard_map/ppermute | solution.py:17
  205.9 2.3 broadcast_select_fusion.1
  208.2 0.5 pad_maximum_fusion
  208.6 0.0 copy-done
  208.7 1.0 fusion.9
  209.7 1.4 collective-permute-start.3
  211.1 4.0 %collective-permute-done.3 = bf16[160,512]{1,0:T(8,128)(2,1)S(1)} collective-permute-done((bf16[160,512]{1,0:T(8,128)(2,1)S(1)}, bf16[160,512]{1,0:T(8,128)(2,1)S(1)}, u32[]{:S(2)}, u32[]{:S(2)}) %collective-permute-start.3) | collective-permute-done | bytes 163872 | tf_op jit(solution)/shard_map/ppermute | solution.py:35
  215.1 0.9 gather_fusion
  216.0 0.0 all-gather.3.cloned.1.call-done
  216.0 8.1 %convolution_convert_fusion = bf16[160,5120]{1,0:T(8,128)(2,1)} fusion(bf16[1,5120,512]{2,1,0:T(8,128)(2,1)} %all-gather.3.cloned.1.call-done, bf16[1,160,5120]{2,1,0:T(8,128)(2,1)S(1)} %copy-done, bf16[160,512]{1,0:T(8,128)(2,1)S(1)} %gather_fusion, pred[160]{0:T(512)(128)(4,1)S(1)} %compare_and_fusion), kind=kOutput, calls=%fused_computation.1 | convolution fusion | flops 1678868480 | bytes 8683680 | tf_op jit(solution)/shard_map/dot_general | solution.py:49
  224.1 0.0 reduce-scatter.2.cloned.1.call-update
  224.1 27.7 %reduce-scatter.2.cloned.1.call-done = bf16[160,2560]{1,0:T(8,128)(2,1)} async-done(((bf16[160,5120]{1,0:T(8,128)(2,1)}), bf16[160,2560]{1,0:T(8,128)(2,1)}) %reduce-scatter.2.cloned.1.call-update) | async-done | bytes 819216 | tf_op jit(solution)/shard_map/reduce_scatter | solution.py:52
  (3 shorter events, 0.0 us)
Async XLA Ops:
  6.5 202.1 %copy-start = (bf16[1,160,5120]{2,1,0:T(8,128)(2,1)S(1)}, bf16[1,160,5120]{2,1,0:T(8,128)(2,1)}, u32[]{:S(2)}) copy-start(bf16[1,160,5120]{2,1,0:T(8,128)(2,1)} %param.4) | copy-start | bytes 4915204
  6.5 209.5 %all-gather.3.cloned.1.call-start = ((), (), s32[]{:S(2)}) async-start(), calls=%async_computation.2 | async-start | bytes 5898240 | tf_op jit(solution)/shard_map/all_gather | solution.py:40
  7.3 244.5 %reduce-scatter.2.cloned.1.call-start = ((), (), s32[]{:S(2)}) async-start(), calls=%async_computation.1 | async-start | bytes 2457600 | tf_op jit(solution)/shard_map/reduce_scatter | solution.py:52
  7.3 2.5 collective-permute-start
  10.9 0.8 copy-start.2
  10.9 1.0 copy-start.3
  12.0 74.3 %collective-permute-start.1 = (bf16[2,640,512]{2,1,0:T(8,128)(2,1)S(1)}, bf16[2,640,512]{2,1,0:T(8,128)(2,1)}, u32[]{:S(2)}, u32[]{:S(2)}) collective-permute-start(bf16[2,640,512]{2,1,0:T(8,128)(2,1)S(1)} %pad_maximum_fusion.2), channel_id=1, source_target_pairs={{0,4},{2,6},{4,0},{6,2},{8,12},{10,14},{12,8},{14,10},{1,5},{3,7},... | collective-permute-start | bytes 3932168 | tf_op jit(solution)/shard_map/ppermute | solution.py:17
  88.1 2.0 copy-start.1
  88.1 3.7 %copy-start.4 = (s32[1,160]{1,0:T(1,128)S(1)}, s32[1,160]{1,0:T(1,128)}, u32[]{:S(2)}) copy-start(s32[1,160]{1,0:T(1,128)} %param.7) | copy-start | bytes 1924
  90.1 115.8 %collective-permute-start.2 = (bf16[4,640,512]{2,1,0:T(8,128)(2,1)}, bf16[4,640,512]{2,1,0:T(8,128)(2,1)}, u32[]{:S(2)}, u32[]{:S(2)}) collective-permute-start(bf16[4,640,512]{2,1,0:T(8,128)(2,1)} %pad_maximum_fusion.1), channel_id=1, source_target_pairs={{0,8},{2,10},{4,12},{6,14},{8,0},{10,2},{12,4},{14,6},{1,9},{3,11}... | collective-permute-start | bytes 7864328 | tf_op jit(solution)/shard_map/ppermute | solution.py:17
  209.7 5.4 %collective-permute-start.3 = (bf16[160,512]{1,0:T(8,128)(2,1)S(1)}, bf16[160,512]{1,0:T(8,128)(2,1)S(1)}, u32[]{:S(2)}, u32[]{:S(2)}) collective-permute-start(bf16[160,512]{1,0:T(8,128)(2,1)S(1)} %fusion.9), channel_id=1, source_target_pairs={{0,16},{16,0},{1,17},{17,1},{2,18},{18,2},{3,19},{19,3},{4,20},{20... | collective-permute-start | bytes 491528 | tf_op jit(solution)/shard_map/ppermute | solution.py:35
Sparse Core Ops, SparseCore 0:
  9.0 78.2 all-gather.2
  224.2 27.5 reduce-scatter.1
